TPU v7x, 32 devices: a whole 2x2x4 slice. The times are simulated.
32 devices in a mesh: blk: 2 (over y), tm: 4 (over z), fsdp: 4 (over x, core).
Axes of the slice: x: 2, y: 2, z: 4, core: 2. Of those that a mesh axis runs over, the one named last changes fastest.
Arguments:
- features: bfloat16 [4, 4, 320, 512], P('fsdp', 'tm', 'blk'), may hold values from -6 to 6
- neighbours: int32 [320, 8], P('blk'), may hold values from 0 to 319, as said below
- conv_taps: float32 [9, 512], replicated, may hold values from -3 to 3
- norm_gain: float32 [512], replicated, may hold values from 0.25 to 1.75
- qkv_weight: bfloat16 [512, 1536], P('fsdp'), as said below
- out_weight: bfloat16 [512, 512], P('fsdp'), may hold values from -0.25 to 0.25
- cotangent: bfloat16 [4, 4, 320, 512], P('fsdp', 'tm', 'blk'), may hold values from -0.083496094 to 0.083496094
Outputs:
- weight_grads: float32 [1048576], P(('blk', 'tm', 'fsdp'))
Inputs may be any that keep to these rules, and one draw needn't show every extreme that they name: `neighbours`: row p holds p - 1, p + 1, three neighbouring pixels near p - 128 and three near p + 128, clipped to the window; every entry lies within 130 of p, and one lies exactly 130 away. `qkv_weight`: projection weights of order 512 ** -0.5 per entry.
All inputs are finite; a program needn't handle non-finite values.
Results may differ from a plain program's by a relative error of at most 0.0086.
Values may be sent and summed in bfloat16 or wider, within the bound.
No kernel may reach another device: no remote copies, remote signals or barrier semaphores. Data moves between devices by JAX's collectives and lax.ppermute only.
A program may use at most 64 MiB of HBM per device.

v0:
```python
import jax
import jax.numpy as jnp
from jax import lax
from jax.sharding import PartitionSpec as P

HEADS = 8
HALO = 130


def with_halo(cells, sides, width):
    for axis, dim in sides:
        count = lax.axis_size(axis)
        ends = count - 1
        head = lax.slice_in_dim(cells, 0, width, axis=dim)
        tail = lax.slice_in_dim(cells, cells.shape[dim] - width, cells.shape[dim], axis=dim)
        cells = jnp.concatenate(
            [
                lax.ppermute(tail, axis, [(i, (i + 1) % count) for i in range(ends)]),
                cells,
                lax.ppermute(head, axis, [((i + 1) % count, i) for i in range(ends)]),
            ],
            axis=dim,
        )
    return cells


def rounded(values):
    return lax.optimization_barrier(values.astype(jnp.bfloat16)).astype(jnp.float32)


def attend_all(qkv_rows, grad_rows):
    frames, pixels, width = qkv_rows.shape
    channels = width // 3

    def split_heads(block):
        return block.reshape(frames, pixels, HEADS, channels // HEADS).astype(jnp.float32)

    queries = split_heads(qkv_rows[:, :, :channels])
    keys_all = split_heads(qkv_rows[:, :, channels : 2 * channels])
    values = split_heads(qkv_rows[:, :, 2 * channels :])
    grads = split_heads(grad_rows)
    scores = jnp.einsum("tpeh,upeh->petu", queries, keys_all) * 0.125
    causal = jnp.arange(frames)[:, None] >= jnp.arange(frames)[None, :]
    masked = jnp.where(causal, scores, -1e30)
    largest = jnp.max(masked, axis=-1, keepdims=True)
    totals = jnp.sum(jnp.exp(masked - largest), axis=-1, keepdims=True)
    log_total = largest + jnp.log(totals)
    weights = rounded(jnp.exp(masked - log_total))
    attended = jnp.einsum("petu,upeh->tpeh", weights, values)
    dprob = jnp.einsum("tpeh,upeh->petu", grads, values)
    delta = jnp.sum(weights * dprob, axis=-1, keepdims=True)
    dscore = rounded(weights * (dprob - delta) * 0.125)
    grad_query = jnp.einsum("petu,upeh->tpeh", dscore, keys_all)
    grad_key = jnp.einsum("petu,tpeh->upeh", dscore, queries)
    grad_value = jnp.einsum("petu,tpeh->upeh", weights, grads)
    joined = jnp.concatenate(
        [part.reshape(frames, pixels, channels) for part in (grad_query, grad_key, grad_value)],
        axis=-1,
    )
    return (
        attended.reshape(frames, pixels, channels).astype(jnp.bfloat16),
        joined.astype(jnp.bfloat16),
    )


def per_device(features, neighbours, conv_taps, norm_gain, qkv_weight, out_weight, cotangent):
    inputs = features[0, 0]
    upstream = cotangent[0, 0]
    pixels, channels = inputs.shape
    padded = with_halo(inputs, (("blk", 0),), HALO)
    first_pixel = lax.axis_index("blk") * pixels
    local_rows = neighbours - first_pixel + HALO
    inputs_f = inputs.astype(jnp.float32)
    spatial = conv_taps[0] * inputs_f
    for column in range(8):
        spatial = spatial + conv_taps[column + 1] * jnp.take(
            padded, local_rows[:, column], axis=0
        ).astype(jnp.float32)
    hidden_f = rounded(inputs_f + spatial)
    inverse = lax.rsqrt(jnp.mean(hidden_f * hidden_f, axis=-1, keepdims=True) + 1e-05)
    normed = (hidden_f * inverse * norm_gain).astype(jnp.bfloat16)
    full_qkv, full_out = (
        lax.all_gather(qkv_weight, "fsdp", axis=0, tiled=True),
        lax.all_gather(out_weight, "fsdp", axis=0, tiled=True),
    )
    att_grads = jnp.dot(upstream, full_out.T, preferred_element_type=jnp.float32).astype(
        jnp.bfloat16
    )
    swap_normed, swap_grads, swap_upstream = (
        lax.all_to_all(normed[None], "tm", split_axis=1, concat_axis=0, tiled=True),
        lax.all_to_all(att_grads[None], "tm", split_axis=1, concat_axis=0, tiled=True),
        lax.all_to_all(upstream[None], "tm", split_axis=1, concat_axis=0, tiled=True),
    )
    frames = swap_normed.shape[0]
    few_pixels = swap_normed.shape[1]
    flat_normed = swap_normed.reshape(-1, channels)
    qkv_rows = jnp.dot(flat_normed, full_qkv, preferred_element_type=jnp.float32).astype(
        jnp.bfloat16
    )
    qkv_rows = qkv_rows.reshape(frames, few_pixels, 3 * channels)
    attended_x, dqkv_x = attend_all(qkv_rows, swap_grads)
    grad_in = jnp.einsum(
        "pc,pd->cd",
        flat_normed,
        dqkv_x.reshape(-1, 3 * channels),
        preferred_element_type=jnp.float32,
    )
    grad_out = jnp.einsum(
        "pc,pd->cd",
        attended_x.reshape(-1, channels),
        swap_upstream.reshape(-1, channels),
        preferred_element_type=jnp.float32,
    )
    summands = jnp.concatenate([grad_in.reshape(-1), grad_out.reshape(-1)])
    return lax.psum_scatter(summands, ("blk", "tm", "fsdp"), scatter_dimension=0, tiled=True)


def solution(mesh):
    return jax.shard_map(
        per_device,
        mesh=mesh,
        in_specs=(
            P("fsdp", "tm", "blk", None),
            P("blk", None),
            P(),
            P(),
            P("fsdp", None),
            P("fsdp", None),
            P("fsdp", "tm", "blk", None),
        ),
        out_specs=P(("blk", "tm", "fsdp")),
        check_vma=False,
    )
```

profile of v0, /device:TPU:0, one launch (start us, length us, event | category | flops | bytes accessed | tf_op | source)
XLA Modules:
  0.0 233.5 jit_solution(5854027250937164633)
XLA Ops:
  6.6 1.1 slice_bitcast_fusion.1
  7.6 4.9 %collective-permute-start = (bf16[130,512]{1,0:T(8,128)(2,1)S(1)}, bf16[130,512]{1,0:T(8,128)(2,1)S(1)}, u32[]{:S(2)}, u32[]{:S(2)}) collective-permute-start(bf16[130,512]{1,0:T(8,128)(2,1)S(1)} %get-tuple-element.9), channel_id=1, source_target_pairs={{0,16},{1,17},{2,18},{3,19},{4,20},{5,21},{6,22},{7,23},{8,24},{9,... | collective-permute-start | bytes 399368 | tf_op jit(solution)/shard_map/ppermute | solution.py:18
  12.6 1.3 collective-permute-start.1
  13.9 7.4 %all_gather.7 = bf16[512,512]{1,0:T(8,128)(2,1)S(1)} all-gather(bf16[128,512]{1,0:T(8,128)(2,1)} %param.14), channel_id=1, replica_groups=mesh['blk'=2,'tm'=4,'fsdp'=4] {'fsdp'}, dimensions={0}, use_global_device_ids=true | all-gather | bytes 655360 | tf_op jit(solution)/shard_map/all_gather | solution.py:84
  21.3 1.2 fusion.10
  23.3 1.6 reduce.4
  25.6 4.9 %all-to-all-start.1 = ((bf16[4,2,10240]{2,1,0:T(2,128)(2,1)}), bf16[4,2,10240]{2,1,0:T(2,128)(2,1)S(1)}, u32[]{:S(2)}, u32[]{:S(2)}) async-start(bf16[4,2,10240]{2,1,0:T(2,128)(2,1)} %reshape.184), calls=%async_computation.1 | async-start | bytes 327680 | tf_op jit(solution)/shard_map/all_to_all | solution.py:91
  31.1 1.6 reduce.3
  33.5 0.9 gather_fusion.2
  34.5 0.9 gather_fusion.3
  35.4 0.9 gather_fusion.4
  36.3 0.9 gather_fusion.5
  37.3 0.9 gather_fusion.6
  38.2 0.9 gather_fusion.7
  39.1 0.9 gather_fusion
  40.1 0.9 gather_fusion.1
  41.6 5.1 %all-to-all-start.2 = ((bf16[4,2,10240]{2,1,0:T(2,128)(2,1)}), bf16[4,2,10240]{2,1,0:T(2,128)(2,1)S(1)}, u32[]{:S(2)}, u32[]{:S(2)}) async-start(bf16[4,2,10240]{2,1,0:T(2,128)(2,1)} %reshape.182), calls=%async_computation.2 | async-start | bytes 327680 | tf_op jit(solution)/shard_map/all_to_all | solution.py:92
  47.1 1.6 reduce.2
  49.4 3.7 %all-to-all-done.2 = bf16[4,2,10240]{2,1,0:T(2,128)(2,1)S(1)} async-done(((bf16[4,2,10240]{2,1,0:T(2,128)(2,1)}), bf16[4,2,10240]{2,1,0:T(2,128)(2,1)S(1)}, u32[]{:S(2)}, u32[]{:S(2)}) %all-to-all-start.2) | async-done | bytes 163872 | tf_op jit(solution)/shard_map/all_to_all | solution.py:92
  53.2 3.3 %all-to-all-start = ((bf16[4,2,10240]{2,1,0:T(2,128)(2,1)}), bf16[4,2,10240]{2,1,0:T(2,128)(2,1)S(1)}, u32[]{:S(2)}, u32[]{:S(2)}) async-start(bf16[4,2,10240]{2,1,0:T(2,128)(2,1)} %reshape.180), calls=%async_computation | async-start | bytes 327680 | tf_op jit(solution)/shard_map/all_to_all | solution.py:90
  56.9 0.9 bitcast_reduce_fusion
  58.0 0.9 reshape.183
  58.9 3.6 %all-to-all-done = bf16[4,2,10240]{2,1,0:T(2,128)(2,1)S(1)} async-done(((bf16[4,2,10240]{2,1,0:T(2,128)(2,1)}), bf16[4,2,10240]{2,1,0:T(2,128)(2,1)S(1)}, u32[]{:S(2)}, u32[]{:S(2)}) %all-to-all-start) | async-done | bytes 163872 | tf_op jit(solution)/shard_map/all_to_all | solution.py:90
  62.7 1.8 convolution_convert_fusion
  69.5 1.3 fusion.9
  71.7 2.3 fusion.12
  74.0 2.7 %reshape.88 = f32[786432]{0:T(1024)S(1)} reshape(f32[512,1536]{1,0:T(8,128)} %fusion.12) | data formatting | bytes 6291456 | tf_op jit(solution)/shard_map/reshape | solution.py:114
  76.6 1.0 copy.55
  78.5 1.4 convolution_bitcast_fusion
  80.2 2.2 pad_maximum_fusion
  82.5 142.6 %all-reduce.3.cloned.1.call-done = f32[1048576]{0:T(1024)} async-done(((f32[1048576]{0:T(1024)}), f32[1048576]{0:T(1024)}) %all-reduce.3.cloned.1.call-update) | async-done | bytes 4194320
  225.1 1.6 dynamic-slice
  (78 shorter events, 12.2 us)
Async XLA Ops:
  6.5 26.9 %copy-start = (bf16[1,1,160,512]{3,2,1,0:T(8,128)(2,1)S(1)}, bf16[1,1,160,512]{3,2,1,0:T(8,128)(2,1)}, u32[]{:S(2)}) copy-start(bf16[1,1,160,512]{3,2,1,0:T(8,128)(2,1)} %param.9) | copy-start | bytes 491524
  6.5 24.3 %copy-start.1 = (bf16[1,1,160,512]{3,2,1,0:T(8,128)(2,1)S(1)}, bf16[1,1,160,512]{3,2,1,0:T(8,128)(2,1)}, u32[]{:S(2)}) copy-start(bf16[1,1,160,512]{3,2,1,0:T(8,128)(2,1)} %param.15) | copy-start | bytes 491524
  6.5 23.9 %copy-start.3 = (s32[160,8]{0,1:T(8,128)S(1)}, s32[160,8]{0,1:T(8,128)}, u32[]{:S(2)}) copy-start(s32[160,8]{0,1:T(8,128)} %param.10) | copy-start | bytes 15364
  6.5 24.2 %copy-start.2 = (f32[9,512]{1,0:T(8,128)S(1)}, f32[9,512]{1,0:T(8,128)}, u32[]{:S(2)}) copy-start(f32[9,512]{1,0:T(8,128)} %param.11) | copy-start | bytes 55300
  6.5 56.1 %all-gather.2.cloned.1.call-start = ((), (), s32[]{:S(2)}) async-start(), calls=%async_computation.3 | async-start | bytes 1966080 | tf_op jit(solution)/shard_map/all_gather | solution.py:83
  7.6 25.8 %collective-permute-start = (bf16[130,512]{1,0:T(8,128)(2,1)S(1)}, bf16[130,512]{1,0:T(8,128)(2,1)S(1)}, u32[]{:S(2)}, u32[]{:S(2)}) collective-permute-start(bf16[130,512]{1,0:T(8,128)(2,1)S(1)} %get-tuple-element.9), channel_id=1, source_target_pairs={{0,16},{1,17},{2,18},{3,19},{4,20},{5,21},{6,22},{7,23},{8,24},{9,... | collective-permute-start | bytes 399368 | tf_op jit(solution)/shard_map/ppermute | solution.py:18
  12.6 20.9 %collective-permute-start.1 = (bf16[130,512]{1,0:T(8,128)(2,1)S(1)}, bf16[130,512]{1,0:T(8,128)(2,1)S(1)}, u32[]{:S(2)}, u32[]{:S(2)}) collective-permute-start(bf16[130,512]{1,0:T(8,128)(2,1)S(1)} %get-tuple-element.10), channel_id=1, source_target_pairs={{16,0},{17,1},{18,2},{19,3},{20,4},{21,5},{22,6},{23,7},{24,8},{25... | collective-permute-start | bytes 399368 | tf_op jit(solution)/shard_map/ppermute | solution.py:20
  25.6 16.0 %all-to-all-start.1 = ((bf16[4,2,10240]{2,1,0:T(2,128)(2,1)}), bf16[4,2,10240]{2,1,0:T(2,128)(2,1)S(1)}, u32[]{:S(2)}, u32[]{:S(2)}) async-start(bf16[4,2,10240]{2,1,0:T(2,128)(2,1)} %reshape.184), calls=%async_computation.1 | async-start | bytes 327680 | tf_op jit(solution)/shard_map/all_to_all | solution.py:91
  38.2 8.6 %copy-start.4 = (f32[512]{0:T(512)S(1)}, f32[512]{0:T(512)}, u32[]{:S(2)}) copy-start(f32[512]{0:T(512)} %param.12) | copy-start | bytes 6148
  41.6 11.5 %all-to-all-start.2 = ((bf16[4,2,10240]{2,1,0:T(2,128)(2,1)}), bf16[4,2,10240]{2,1,0:T(2,128)(2,1)S(1)}, u32[]{:S(2)}, u32[]{:S(2)}) async-start(bf16[4,2,10240]{2,1,0:T(2,128)(2,1)} %reshape.182), calls=%async_computation.2 | async-start | bytes 327680 | tf_op jit(solution)/shard_map/all_to_all | solution.py:92
  53.2 9.3 %all-to-all-start = ((bf16[4,2,10240]{2,1,0:T(2,128)(2,1)}), bf16[4,2,10240]{2,1,0:T(2,128)(2,1)S(1)}, u32[]{:S(2)}, u32[]{:S(2)}) async-start(bf16[4,2,10240]{2,1,0:T(2,128)(2,1)} %reshape.180), calls=%async_computation | async-start | bytes 327680 | tf_op jit(solution)/shard_map/all_to_all | solution.py:90
  56.5 168.6 %all-reduce.3.cloned.1.call-start = ((), (), s32[]{:S(2)}) async-start(), calls=%async_computation.4 | async-start | bytes 8388608
Sparse Core Ops, SparseCore 0:
  14.0 21.9 all-gather.1
  82.6 142.4 all-reduce.2
where the time goes:
time: 234 us
  waiting for transfers between devices  150 us (64%)
  local copies, waits for them, and re-layouts  22.1 us (9%)
  starting transfers between devices  19.8 us (8%)
  between operations  13.9 us (6%)
  matrix products  10.9 us (5%)
  other arithmetic  9.43 us (4%)
  blocking collectives  7.38 us (3%)
    unnamed x3, waiting for transfers between devices  143 us
    gather x8, local copies, waits for them, and re-layouts, per_device(): jnp.take(padded, local_rows[:, column], axis=0).astype(jnp.float32)  7.45 us
    all_gather x1, blocking collectives, per_device(): lax.all_gather(out_weight, 'fsdp', axis=0, tiled=True)  7.38 us
    unnamed x19, local copies, waits for them, and re-layouts  5.73 us
    all_to_all x1, starting transfers between devices, per_device(): lax.all_to_all(upstream[None], 'tm', split_axis=1, concat_axis=0, tiled=T...  5.09 us
    ppermute x1, starting transfers between devices, with_halo(): lax.ppermute(tail, axis, [(i, (i + 1) % count) for i in range(ends)])  4.91 us
    all_to_all x1, starting transfers between devices, per_device(): lax.all_to_all(att_grads[None], 'tm', split_axis=1, concat_axis=0, tiled=...  4.86 us
    unnamed x3, other arithmetic  4.81 us
  transfers between devices with their start and end apart: 7, of which 3 were waited for; matrix products, arithmetic and copies ran while one was open for 9% of the time, Pallas kernels for 0%

commit v1 on v0

--- a/solution.py
+++ b/solution.py
@@ -22,6 +22,30 @@
             axis=dim,
         )
     return cells
+
+
+def halved(partial, axis, bit):
+    count = lax.axis_size(axis)
+    mine = (lax.axis_index(axis) >> bit) & 1
+    keep = lax.dynamic_index_in_dim(partial, mine, 0, keepdims=False)
+    send = lax.dynamic_index_in_dim(partial, 1 - mine, 0, keepdims=False)
+    got = lax.ppermute(send.astype(jnp.bfloat16), axis, [(i, i ^ (1 << bit)) for i in range(count)])
+    return keep + got.astype(jnp.float32)
+
+
+def scattered_sum(summands):
+    counts = [lax.axis_size(axis) for axis in ("blk", "tm", "fsdp")]
+    bits = [count.bit_length() - 1 for count in counts]
+    order = [("fsdp", bit) for bit in range(bits[2])]
+    order += [("blk", bit) for bit in range(bits[0])]
+    order += [("tm", bit) for bit in range(bits[1])]
+    labels = [(axis, bit) for axis, many in zip(("blk", "tm", "fsdp"), bits) for bit in reversed(range(many))]
+    partial = summands.reshape((2,) * len(labels) + (-1, 128))
+    for axis, bit in order:
+        place = labels.index((axis, bit))
+        labels.pop(place)
+        partial = halved(jnp.moveaxis(partial, place, 0), axis, bit)
+    return partial.reshape(-1)
 
 
 def rounded(values):
@@ -112,7 +136,7 @@
         preferred_element_type=jnp.float32,
     )
     summands = jnp.concatenate([grad_in.reshape(-1), grad_out.reshape(-1)])
-    return lax.psum_scatter(summands, ("blk", "tm", "fsdp"), scatter_dimension=0, tiled=True)
+    return scattered_sum(summands)
 
 
 def solution(mesh):

time: 234 us -> 130 us (0.56)
  waiting for transfers between devices: 150 us -> 36.7 us
  starting transfers between devices: 19.8 us -> 25.9 us
    unnamed x3 -> x1, waiting for transfers between devices: 143 us -> 0.02 us
    ppermute x0 -> x5, waiting for transfers between devices: none -> 29.4 us  [halved(): lax.ppermute(send.astype(jnp.bfloat16), axis, [(i, i ^ 1 << bit) for i in...]
    ppermute x0 -> x5, starting transfers between devices: none -> 6.22 us  [halved(): lax.ppermute(send.astype(jnp.bfloat16), axis, [(i, i ^ 1 << bit) for i in...]
    add x0 -> x4, other arithmetic: none -> 3 us  [halved(): return keep + got.astype(jnp.float32)]
    unnamed x19 -> x20, local copies, waits for them, and re-layouts: 5.73 us -> 6.13 us
  transfers between devices with their start and end apart: 7 -> 11, of which waited for: 3 -> 7; matrix products, arithmetic and copies ran while one was open for 9% -> 16% of each run, Pallas kernels for 0% -> 0%
where the time goes in v1:
time: 130 us; the launch traced here: 129 us
  waiting for transfers between devices  36.7 us (28%)
  starting transfers between devices  25.9 us (20%)
  local copies, waits for them, and re-layouts  22.9 us (18%)
  between operations  14 us (11%)
  other arithmetic  11.1 us (9%)
  matrix products  10.9 us (8%)
  blocking collectives  7.38 us (6%)
    ppermute x5, waiting for transfers between devices, halved(): lax.ppermute(send.astype(jnp.bfloat16), axis, [(i, i ^ 1 << bit) for i in...  29.4 us
    gather x8, local copies, waits for them, and re-layouts, per_device(): jnp.take(padded, local_rows[:, column], axis=0).astype(jnp.float32)  7.45 us
    all_gather x1, blocking collectives, per_device(): lax.all_gather(out_weight, 'fsdp', axis=0, tiled=True)  7.38 us
    ppermute x5, starting transfers between devices, halved(): lax.ppermute(send.astype(jnp.bfloat16), axis, [(i, i ^ 1 << bit) for i in...  6.22 us
    unnamed x20, local copies, waits for them, and re-layouts  6.13 us
    all_to_all x1, starting transfers between devices, per_device(): lax.all_to_all(upstream[None], 'tm', split_axis=1, concat_axis=0, tiled=T...  5.09 us
    ppermute x1, starting transfers between devices, with_halo(): lax.ppermute(tail, axis, [(i, (i + 1) % count) for i in range(ends)])  4.91 us
    all_to_all x1, starting transfers between devices, per_device(): lax.all_to_all(att_grads[None], 'tm', split_axis=1, concat_axis=0, tiled=...  4.86 us
  transfers between devices with their start and end apart: 11, of which 7 were waited for; matrix products, arithmetic and copies ran while one was open for 16% of the time, Pallas kernels for 0%

profile of v1, /device:TPU:0, one launch (start us, length us, event | category | flops | bytes accessed | tf_op | source)
XLA Modules:
  0.0 129.0 jit_solution(17542677905588664984)
XLA Ops:
  6.6 1.1 slice_bitcast_fusion.1
  7.6 4.9 %collective-permute-start = (bf16[130,512]{1,0:T(8,128)(2,1)S(1)}, bf16[130,512]{1,0:T(8,128)(2,1)S(1)}, u32[]{:S(2)}, u32[]{:S(2)}) collective-permute-start(bf16[130,512]{1,0:T(8,128)(2,1)S(1)} %get-tuple-element.9), channel_id=1, source_target_pairs={{0,16},{1,17},{2,18},{3,19},{4,20},{5,21},{6,22},{7,23},{8,24},{9,... | collective-permute-start | bytes 399368 | tf_op jit(solution)/shard_map/ppermute | solution.py:18
  12.6 1.3 %collective-permute-start.1 = (bf16[130,512]{1,0:T(8,128)(2,1)S(1)}, bf16[130,512]{1,0:T(8,128)(2,1)S(1)}, u32[]{:S(2)}, u32[]{:S(2)}) collective-permute-start(bf16[130,512]{1,0:T(8,128)(2,1)S(1)} %get-tuple-element.10), channel_id=1, source_target_pairs={{16,0},{17,1},{18,2},{19,3},{20,4},{21,5},{22,6},{23,7},{24,8},{25... | collective-permute-start | bytes 399368 | tf_op jit(solution)/shard_map/ppermute | solution.py:20
  13.9 7.4 %all_gather.7 = bf16[512,512]{1,0:T(8,128)(2,1)S(1)} all-gather(bf16[128,512]{1,0:T(8,128)(2,1)} %param.14), channel_id=1, replica_groups=mesh['blk'=2,'tm'=4,'fsdp'=4] {'fsdp'}, dimensions={0}, use_global_device_ids=true | all-gather | bytes 655360 | tf_op jit(solution)/shard_map/all_gather | solution.py:108
  21.3 1.2 fusion.10
  23.3 1.6 %reduce.4 = bf16[160,512]{1,0:T(8,128)(2,1)S(1)} reduce(bf16[160,1,512]{2,1,0:T(2,128)(2,1)S(1)} %bitcast.109, bf16[]{:T(256)} %broadcast.56), dimensions={1}, to_apply=%bitcast.102.reduce_sub_computation | reduce | bytes 327682
  25.6 4.9 %all-to-all-start.1 = ((bf16[4,2,10240]{2,1,0:T(2,128)(2,1)}), bf16[4,2,10240]{2,1,0:T(2,128)(2,1)S(1)}, u32[]{:S(2)}, u32[]{:S(2)}) async-start(bf16[4,2,10240]{2,1,0:T(2,128)(2,1)} %reshape.209), calls=%async_computation.1 | async-start | bytes 327680 | tf_op jit(solution)/shard_map/all_to_all | solution.py:115
  31.0 1.6 %reduce.3 = bf16[160,512]{1,0:T(8,128)(2,1)S(1)} reduce(bf16[160,1,512]{2,1,0:T(2,128)(2,1)S(1)} %bitcast.111, bf16[]{:T(256)} %broadcast.56), dimensions={1}, to_apply=%bitcast.101.reduce_sub_computation | reduce | bytes 327682
  33.5 0.9 gather_fusion.2
  38.2 0.9 gather_fusion
  41.6 5.1 %all-to-all-start.2 = ((bf16[4,2,10240]{2,1,0:T(2,128)(2,1)}), bf16[4,2,10240]{2,1,0:T(2,128)(2,1)S(1)}, u32[]{:S(2)}, u32[]{:S(2)}) async-start(bf16[4,2,10240]{2,1,0:T(2,128)(2,1)} %reshape.207), calls=%async_computation.2 | async-start | bytes 327680 | tf_op jit(solution)/shard_map/all_to_all | solution.py:116
  47.1 1.6 %reduce.2 = bf16[160,512]{1,0:T(8,128)(2,1)S(1)} reduce(bf16[160,1,512]{2,1,0:T(2,128)(2,1)S(1)} %bitcast.110, bf16[]{:T(256)} %broadcast.56), dimensions={1}, to_apply=%bitcast.103.reduce_sub_computation | reduce | bytes 327682
  49.4 3.7 %all-to-all-done.2 = bf16[4,2,10240]{2,1,0:T(2,128)(2,1)S(1)} async-done(((bf16[4,2,10240]{2,1,0:T(2,128)(2,1)}), bf16[4,2,10240]{2,1,0:T(2,128)(2,1)S(1)}, u32[]{:S(2)}, u32[]{:S(2)}) %all-to-all-start.2) | async-done | bytes 163872 | tf_op jit(solution)/shard_map/all_to_all | solution.py:116
  53.1 3.5 %all-to-all-start = ((bf16[4,2,10240]{2,1,0:T(2,128)(2,1)}), bf16[4,2,10240]{2,1,0:T(2,128)(2,1)S(1)}, u32[]{:S(2)}, u32[]{:S(2)}) async-start(bf16[4,2,10240]{2,1,0:T(2,128)(2,1)} %reshape.205), calls=%async_computation | async-start | bytes 327680 | tf_op jit(solution)/shard_map/all_to_all | solution.py:114
  58.8 3.6 %all-to-all-done = bf16[4,2,10240]{2,1,0:T(2,128)(2,1)S(1)} async-done(((bf16[4,2,10240]{2,1,0:T(2,128)(2,1)}), bf16[4,2,10240]{2,1,0:T(2,128)(2,1)S(1)}, u32[]{:S(2)}, u32[]{:S(2)}) %all-to-all-start) | async-done | bytes 163872 | tf_op jit(solution)/shard_map/all_to_all | solution.py:114
  62.6 1.8 %convolution_convert_fusion = bf16[160,1536]{1,0:T(8,128)(2,1)S(1)} fusion(bf16[512,1536]{1,0:T(8,128)(2,1)} %all-gather.2.cloned.1.call-done, bf16[1,160,512]{2,0,1:T(2,128)(2,1)S(1)} %bitcast.112), kind=kOutput, calls=%fused_computation.10 | convolution fusion | flops 251904000 | bytes 2228224 | tf_op jit(solution)/shard_map/dot_general | solution.py:121
  69.5 1.3 %fusion.9 = bf16[4,40,8,64]{3,0,2,1:T(4,128)(2,1)} fusion(bf16[40,8,4,4]{2,3,1,0:T(4,128)(2,1)S(1)} %exponential_convert_fusion, bf16[4,40,8,64]{3,2,1,0:T(8,128)(2,1)S(1)} %reshape.110), kind=kOutput, calls=%fused_computation.27 | convolution fusion | flops 737280 | bytes 337920 | tf_op jit(solution)/shard_map/petu,upeh->tpeh/dot_general | solution.py:73
  71.7 2.2 %fusion.14 = f32[512,1536]{1,0:T(8,128)} fusion(bf16[160,512]{1,0:T(8,128)(2,1)S(1)} %concatenate.20, bf16[160,512]{1,0:T(8,128)(2,1)S(1)} %concatenate.19, bf16[160,512]{1,0:T(8,128)(2,1)S(1)} %concatenate.18, bf16[1,160,512]{2,0,1:T(2,128)(2,1)S(1)} %bitcast.113), kind=kOutput, calls=%fused_computation.40 | convolution fusion | flops 253132800 | bytes 3801088 | tf_op jit(solution)/shard_map/pc,pd->cd/dot_general | solution.py:126
  73.9 2.7 %reshape.111 = f32[786432]{0:T(1024)S(1)} reshape(f32[512,1536]{1,0:T(8,128)} %fusion.14) | data formatting | bytes 6291456 | tf_op jit(solution)/shard_map/reshape | solution.py:138
  76.6 1.0 copy.55
  78.5 1.4 %convolution_bitcast_fusion = f32[64,4,8,128]{3,2,1,0:T(8,128)S(1)} fusion(bf16[160,512]{1,0:T(8,128)(2,1)} %convert_element_type.132, bf16[1,160,512]{2,0,1:T(2,128)(2,1)} %bitcast.114), kind=kOutput, calls=%fused_computation.13 | convolution fusion | flops 83886080 | bytes 1376256 | tf_op jit(solution)/shard_map/pc,pd->cd/dot_general | solution.py:132
  80.5 1.9 %copy-done = f32[1048576]{0:T(1024)} copy-done((f32[1048576]{0:T(1024)}, f32[1048576]{0:T(1024)S(1)}, u32[]{:S(2)}) %copy-start) | copy-done | bytes 4194328
  82.7 2.6 %collective-permute-done.2 = bf16[2,2,2,2,256,128]{5,4,3,2,1,0:T(8,128)(2,1)S(1)} collective-permute-done((bf16[2,2,2,2,256,128]{5,4,3,2,1,0:T(8,128)(2,1)S(1)}, bf16[2,2,2,2,256,128]{5,4,3,2,1,0:T(8,128)(2,1)S(1)}, u32[]{:S(2)}, u32[]{:S(2)}) %collective-permute-start.2) | collective-permute-done | bytes 1048608 | tf_op jit(solution)/shard_map/ppermute | solution.py:32
  85.3 1.8 %bitcast_add_fusion = f32[2,2,2,2,256,128]{5,4,3,2,1,0:T(8,128)S(1)} fusion(bf16[2,2,2,2,256,128]{5,4,3,2,1,0:T(8,128)(2,1)S(1)} %collective-permute-done.2, f32[2,2,2,2,2,256,128]{6,5,4,3,2,1,0:T(8,128)} %bitcast.105, s32[]{:T(128)S(6)} %select_n.47), kind=kLoop, calls=%fused_computation.11 | loop fusion | flops 1048576 | bytes 5242884 | tf_op jit(solution)/shard_map/add | solution.py:33
  88.1 13.3 %collective-permute-done.3 = bf16[2,2,2,256,128]{4,3,2,1,0:T(8,128)(2,1)} collective-permute-done((bf16[2,2,2,256,128]{4,3,2,1,0:T(8,128)(2,1)S(1)}, bf16[2,2,2,256,128]{4,3,2,1,0:T(8,128)(2,1)}, u32[]{:S(2)}, u32[]{:S(2)}) %collective-permute-start.3) | collective-permute-done | bytes 524320 | tf_op jit(solution)/shard_map/ppermute | solution.py:32
  101.4 1.1 bitcast_add_fusion.1
  102.6 2.7 %collective-permute-start.4 = (bf16[2,2,256,128]{3,2,1,0:T(8,128)(2,1)S(1)}, bf16[2,2,256,128]{3,2,1,0:T(8,128)(2,1)S(1)}, u32[]{:S(2)}, u32[]{:S(2)}) collective-permute-start(bf16[2,2,256,128]{3,2,1,0:T(8,128)(2,1)S(1)} %fusion.32), channel_id=1, source_target_pairs={{0,16},{16,0},{1,17},{17,1},{2,18},{18,2},{3,19},{19,3},{4,20},{20... | collective-permute-start | bytes 786440 | tf_op jit(solution)/shard_map/ppermute | solution.py:32
  105.3 5.8 %collective-permute-done.4 = bf16[2,2,256,128]{3,2,1,0:T(8,128)(2,1)S(1)} collective-permute-done((bf16[2,2,256,128]{3,2,1,0:T(8,128)(2,1)S(1)}, bf16[2,2,256,128]{3,2,1,0:T(8,128)(2,1)S(1)}, u32[]{:S(2)}, u32[]{:S(2)}) %collective-permute-start.4) | collective-permute-done | bytes 262176 | tf_op jit(solution)/shard_map/ppermute | solution.py:32
  111.1 1.5 %collective-permute-start.5 = (bf16[2,256,128]{2,1,0:T(8,128)(2,1)S(1)}, bf16[2,256,128]{2,1,0:T(8,128)(2,1)S(1)}, u32[]{:S(2)}, u32[]{:S(2)}) collective-permute-start(bf16[2,256,128]{2,1,0:T(8,128)(2,1)S(1)} %fusion.48), channel_id=1, source_target_pairs={{0,4},{4,0},{8,12},{12,8},{1,5},{5,1},{9,13},{13,9},{2,6},{6,2},{1... | collective-permute-start | bytes 393224 | tf_op jit(solution)/shard_map/ppermute | solution.py:32
  112.6 3.5 %collective-permute-done.5 = bf16[2,256,128]{2,1,0:T(8,128)(2,1)S(1)} collective-permute-done((bf16[2,256,128]{2,1,0:T(8,128)(2,1)S(1)}, bf16[2,256,128]{2,1,0:T(8,128)(2,1)S(1)}, u32[]{:S(2)}, u32[]{:S(2)}) %collective-permute-start.5) | collective-permute-done | bytes 131104 | tf_op jit(solution)/shard_map/ppermute | solution.py:32
  116.2 1.1 collective-permute-start.6
  117.3 4.2 %collective-permute-done.6 = bf16[256,128]{1,0:T(8,128)(2,1)S(1)} collective-permute-done((bf16[256,128]{1,0:T(8,128)(2,1)S(1)}, bf16[256,128]{1,0:T(8,128)(2,1)S(1)}, u32[]{:S(2)}, u32[]{:S(2)}) %collective-permute-start.6) | collective-permute-done | bytes 65568 | tf_op jit(solution)/shard_map/ppermute | solution.py:32
  (92 shorter events, 21.7 us)
Async XLA Ops:
  6.5 26.9 %copy-start.1 = (bf16[1,1,160,512]{3,2,1,0:T(8,128)(2,1)S(1)}, bf16[1,1,160,512]{3,2,1,0:T(8,128)(2,1)}, u32[]{:S(2)}) copy-start(bf16[1,1,160,512]{3,2,1,0:T(8,128)(2,1)} %param.9) | copy-start | bytes 491524
  6.5 24.2 %copy-start.2 = (bf16[1,1,160,512]{3,2,1,0:T(8,128)(2,1)S(1)}, bf16[1,1,160,512]{3,2,1,0:T(8,128)(2,1)}, u32[]{:S(2)}) copy-start(bf16[1,1,160,512]{3,2,1,0:T(8,128)(2,1)} %param.15) | copy-start | bytes 491524
  6.5 23.9 %copy-start.4 = (s32[160,8]{0,1:T(8,128)S(1)}, s32[160,8]{0,1:T(8,128)}, u32[]{:S(2)}) copy-start(s32[160,8]{0,1:T(8,128)} %param.10) | copy-start | bytes 15364
  6.5 24.2 %copy-start.3 = (f32[9,512]{1,0:T(8,128)S(1)}, f32[9,512]{1,0:T(8,128)}, u32[]{:S(2)}) copy-start(f32[9,512]{1,0:T(8,128)} %param.11) | copy-start | bytes 55300
  6.5 56.1 %all-gather.2.cloned.1.call-start = ((), (), s32[]{:S(2)}) async-start(), calls=%async_computation.3 | async-start | bytes 1966080 | tf_op jit(solution)/shard_map/all_gather | solution.py:107
  7.6 25.8 %collective-permute-start = (bf16[130,512]{1,0:T(8,128)(2,1)S(1)}, bf16[130,512]{1,0:T(8,128)(2,1)S(1)}, u32[]{:S(2)}, u32[]{:S(2)}) collective-permute-start(bf16[130,512]{1,0:T(8,128)(2,1)S(1)} %get-tuple-element.9), channel_id=1, source_target_pairs={{0,16},{1,17},{2,18},{3,19},{4,20},{5,21},{6,22},{7,23},{8,24},{9,... | collective-permute-start | bytes 399368 | tf_op jit(solution)/shard_map/ppermute | solution.py:18
  12.6 20.8 %collective-permute-start.1 = (bf16[130,512]{1,0:T(8,128)(2,1)S(1)}, bf16[130,512]{1,0:T(8,128)(2,1)S(1)}, u32[]{:S(2)}, u32[]{:S(2)}) collective-permute-start(bf16[130,512]{1,0:T(8,128)(2,1)S(1)} %get-tuple-element.10), channel_id=1, source_target_pairs={{16,0},{17,1},{18,2},{19,3},{20,4},{21,5},{22,6},{23,7},{24,8},{25... | collective-permute-start | bytes 399368 | tf_op jit(solution)/shard_map/ppermute | solution.py:20
  25.6 16.0 %all-to-all-start.1 = ((bf16[4,2,10240]{2,1,0:T(2,128)(2,1)}), bf16[4,2,10240]{2,1,0:T(2,128)(2,1)S(1)}, u32[]{:S(2)}, u32[]{:S(2)}) async-start(bf16[4,2,10240]{2,1,0:T(2,128)(2,1)} %reshape.209), calls=%async_computation.1 | async-start | bytes 327680 | tf_op jit(solution)/shard_map/all_to_all | solution.py:115
  38.2 8.6 %copy-start.5 = (f32[512]{0:T(512)S(1)}, f32[512]{0:T(512)}, u32[]{:S(2)}) copy-start(f32[512]{0:T(512)} %param.12) | copy-start | bytes 6148
  41.6 11.5 %all-to-all-start.2 = ((bf16[4,2,10240]{2,1,0:T(2,128)(2,1)}), bf16[4,2,10240]{2,1,0:T(2,128)(2,1)S(1)}, u32[]{:S(2)}, u32[]{:S(2)}) async-start(bf16[4,2,10240]{2,1,0:T(2,128)(2,1)} %reshape.207), calls=%async_computation.2 | async-start | bytes 327680 | tf_op jit(solution)/shard_map/all_to_all | solution.py:116
  53.1 9.3 %all-to-all-start = ((bf16[4,2,10240]{2,1,0:T(2,128)(2,1)}), bf16[4,2,10240]{2,1,0:T(2,128)(2,1)S(1)}, u32[]{:S(2)}, u32[]{:S(2)}) async-start(bf16[4,2,10240]{2,1,0:T(2,128)(2,1)} %reshape.205), calls=%async_computation | async-start | bytes 327680 | tf_op jit(solution)/shard_map/all_to_all | solution.py:114
  80.5 2.0 %copy-start = (f32[1048576]{0:T(1024)}, f32[1048576]{0:T(1024)S(1)}, u32[]{:S(2)}) copy-start(f32[1048576]{0:T(1024)S(1)} %pad_maximum_fusion) | copy-start | bytes 12582916
  82.6 2.7 %collective-permute-start.2 = (bf16[2,2,2,2,256,128]{5,4,3,2,1,0:T(8,128)(2,1)S(1)}, bf16[2,2,2,2,256,128]{5,4,3,2,1,0:T(8,128)(2,1)S(1)}, u32[]{:S(2)}, u32[]{:S(2)}) collective-permute-start(bf16[2,2,2,2,256,128]{5,4,3,2,1,0:T(8,128)(2,1)S(1)} %fusion.11), channel_id=1, source_target_pairs={{0,1},{1,0},{2,3},{3,2},{4,5},{5,4},{6,7},{7,6},{8,9},{9,8},{10,11... | collective-permute-start | bytes 3145736 | tf_op jit(solution)/shard_map/ppermute | solution.py:32
  87.2 14.1 %collective-permute-start.3 = (bf16[2,2,2,256,128]{4,3,2,1,0:T(8,128)(2,1)S(1)}, bf16[2,2,2,256,128]{4,3,2,1,0:T(8,128)(2,1)}, u32[]{:S(2)}, u32[]{:S(2)}) collective-permute-start(bf16[2,2,2,256,128]{4,3,2,1,0:T(8,128)(2,1)S(1)} %fusion.13), channel_id=1, source_target_pairs={{0,2},{1,3},{2,0},{3,1},{4,6},{5,7},{6,4},{7,5},{8,10},{9,11},{10,... | collective-permute-start | bytes 1572872 | tf_op jit(solution)/shard_map/ppermute | solution.py:32
  102.6 8.5 %collective-permute-start.4 = (bf16[2,2,256,128]{3,2,1,0:T(8,128)(2,1)S(1)}, bf16[2,2,256,128]{3,2,1,0:T(8,128)(2,1)S(1)}, u32[]{:S(2)}, u32[]{:S(2)}) collective-permute-start(bf16[2,2,256,128]{3,2,1,0:T(8,128)(2,1)S(1)} %fusion.32), channel_id=1, source_target_pairs={{0,16},{16,0},{1,17},{17,1},{2,18},{18,2},{3,19},{19,3},{4,20},{20... | collective-permute-start | bytes 786440 | tf_op jit(solution)/shard_map/ppermute | solution.py:32
  111.1 5.0 %collective-permute-start.5 = (bf16[2,256,128]{2,1,0:T(8,128)(2,1)S(1)}, bf16[2,256,128]{2,1,0:T(8,128)(2,1)S(1)}, u32[]{:S(2)}, u32[]{:S(2)}) collective-permute-start(bf16[2,256,128]{2,1,0:T(8,128)(2,1)S(1)} %fusion.48), channel_id=1, source_target_pairs={{0,4},{4,0},{8,12},{12,8},{1,5},{5,1},{9,13},{13,9},{2,6},{6,2},{1... | collective-permute-start | bytes 393224 | tf_op jit(solution)/shard_map/ppermute | solution.py:32
  116.2 5.2 %collective-permute-start.6 = (bf16[256,128]{1,0:T(8,128)(2,1)S(1)}, bf16[256,128]{1,0:T(8,128)(2,1)S(1)}, u32[]{:S(2)}, u32[]{:S(2)}) collective-permute-start(bf16[256,128]{1,0:T(8,128)(2,1)S(1)} %fusion.50), channel_id=1, source_target_pairs={{0,8},{4,12},{8,0},{12,4},{1,9},{5,13},{9,1},{13,5},{2,10},{6,14},... | collective-permute-start | bytes 196616 | tf_op jit(solution)/shard_map/ppermute | solution.py:32
Sparse Core Ops, SparseCore 0:
  14.0 21.9 all-gather.1
